TPU v7x, 512 devices: a whole 4x8x8 slice. The times are simulated.
512 devices in a mesh: row: 8 (over z), col: 8 (over x, y_hi), pair: 8 (over y_lo, core).
Axes of the slice: x: 4, y: 8 (y_hi: 2, y_lo: 4; y = y_hi * 4 + y_lo), z: 8, core: 2. Of those that a mesh axis runs over, the one named last changes fastest.
Arguments:
- pair_slab: bfloat16 [3072, 16384], P('pair', 'row'), may hold values from -0.4375 to 0.4375
- pair_weights: float32 [3072], P('pair'), may hold values from 0.2 to 2
Outputs:
- polarizability: float32 [16384, 16384], P('row', ('col', 'pair'))
All inputs are finite; a program needn't handle non-finite values.
Results may differ from a plain program's by a relative error of at most 0.0085.
Values may be sent and summed in bfloat16 or wider, within the bound.
A program may use at most 64 MiB of HBM per device.

v0:
```python
import jax
import jax.numpy as jnp
from jax import lax
from jax.sharding import PartitionSpec as P


def from_root(block, axis, owner):
    block = jnp.where(lax.axis_index(axis) == owner, block, jnp.zeros_like(block))
    return lax.psum(block, axis)


def contract_pairs(left, right):
    return lax.dot_general(
        left, right, (((0,), (0,)), ((), ())), preferred_element_type=jnp.float32
    )


def on_device(pair_slab, pair_weights):
    col_index = lax.axis_index("col")
    column_block = from_root(pair_slab, "row", col_index)
    own_columns = lax.all_to_all(column_block, "pair", split_axis=1, concat_axis=0, tiled=True)
    rows_piece = lax.all_gather(pair_slab, "pair", axis=0, tiled=True)
    weight_piece = lax.all_gather(
        pair_weights.astype(jnp.bfloat16), "pair", axis=0, tiled=True
    ).astype(jnp.float32)
    weighted = (weight_piece[:, None] * rows_piece.astype(jnp.float32)).astype(jnp.bfloat16)
    return contract_pairs(weighted, own_columns)


def solution(mesh):
    placed = (P("pair", "row"), P("pair"))
    return jax.shard_map(
        on_device, mesh=mesh, in_specs=placed, out_specs=P("row", ("col", "pair")), check_vma=False
    )
```

profile of v0, /device:TPU:9, one launch (start us, length us, event | category | flops | bytes accessed | tf_op | source)
XLA Modules:
  0.0 204.4 jit_solution(2897368251389527808)
XLA Ops:
  7.4 0.0 all-reduce.2.cloned.1.call-start
  7.4 1.9 copy.5
  9.3 1.3 broadcast_select_fusion
  10.5 0.0 all-reduce.2.cloned.1.call-update
  10.6 0.0 all-gather.3.cloned.1.call-start
  10.6 0.5 all-gather.3.cloned.1.call-update
  11.2 0.0 copy-start
  11.2 85.3 %all-reduce.2.cloned.1.call-done = bf16[384,8,256]{0,2,1:T(8,128)(2,1)} async-done(((bf16[384,8,256]{0,2,1:T(8,128)(2,1)}), bf16[384,8,256]{0,2,1:T(8,128)(2,1)}) %all-reduce.2.cloned.1.call-update) | async-done | bytes 1572880 | tf_op jit(solution)/shard_map/psum | solution.py:9
  96.5 9.2 %all-to-all-start = ((bf16[384,8,256]{0,2,1:T(8,128)(2,1)}), bf16[384,8,256]{0,2,1:T(8,128)(2,1)S(1)}, u32[]{:S(2)}, u32[]{:S(2)}) async-start(bf16[384,8,256]{0,2,1:T(8,128)(2,1)} %all-reduce.2.cloned.1.call-done), calls=%async_computation | async-start | bytes 3145728 | tf_op jit(solution)/shard_map/all_to_all | solution.py:21
  105.7 0.0 copy-done
  105.7 65.9 %all-gather = bf16[8,1,384]{2,1,0:T(2,128)(2,1)S(1)} all-gather(bf16[1,1,384]{2,1,0:T(2,128)(2,1)S(1)} %reshape.4), channel_id=1, replica_groups=mesh['row'=8,'col'=8,'pair'=8] {'pair'}, dimensions={0}, use_global_device_ids=true | all-gather | bytes 6912 | tf_op jit(solution)/shard_map/all_gather | solution.py:23
  171.6 0.0 all-to-all-done
  171.7 0.8 copy.6
  172.4 13.9 %all-gather.3.cloned.1.call-done = bf16[3072,2048]{1,0:T(8,128)(2,1)} async-done(((bf16[384,2048]{1,0:T(8,128)(2,1)}), bf16[3072,2048]{1,0:T(8,128)(2,1)}) %all-gather.3.cloned.1.call-update) | async-done | bytes 12582928 | tf_op jit(solution)/shard_map/all_gather | solution.py:22
  186.3 10.6 %fusion = f32[2048,256]{1,0:T(8,128)} fusion(bf16[3072,256]{1,0:T(8,128)(2,1)S(1)} %bitcast.7, bf16[3072,2048]{1,0:T(8,128)(2,1)} %all-gather.3.cloned.1.call-done, f32[3072]{0:T(1024)S(1)} %bitcast.8), kind=kOutput, calls=%fused_computation.1 | convolution fusion | flops 3240099840 | bytes 16265216 | tf_op jit(solution)/shard_map/dot_general | solution.py:13
  (3 shorter events, 0.0 us)
Async XLA Ops:
  7.4 89.1 %all-reduce.2.cloned.1.call-start = ((), (), s32[]{:S(2)}) async-start(), calls=%async_computation.2 | async-start | bytes 3145728 | tf_op jit(solution)/shard_map/psum | solution.py:9
  10.6 175.7 %all-gather.3.cloned.1.call-start = ((), (), s32[]{:S(2)}) async-start(), calls=%async_computation.1 | async-start | bytes 14155776 | tf_op jit(solution)/shard_map/all_gather | solution.py:22
  11.2 94.5 %copy-start = (f32[384]{0:T(512)S(1)}, f32[384]{0:T(512)}, u32[]{:S(2)}) copy-start(f32[384]{0:T(512)} %param.3) | copy-start | bytes 4612
  96.5 75.2 %all-to-all-start = ((bf16[384,8,256]{0,2,1:T(8,128)(2,1)}), bf16[384,8,256]{0,2,1:T(8,128)(2,1)S(1)}, u32[]{:S(2)}, u32[]{:S(2)}) async-start(bf16[384,8,256]{0,2,1:T(8,128)(2,1)} %all-reduce.2.cloned.1.call-done), calls=%async_computation | async-start | bytes 3145728 | tf_op jit(solution)/shard_map/all_to_all | solution.py:21
Sparse Core Ops, SparseCore 0:
  10.7 85.7 all-reduce.1
Sparse Core Ops, SparseCore 1:
  13.1 173.1 all-gather.2
where the time goes:
time: 205 us; the launch traced here: 204 us
  waiting for transfers between devices  99.8 us (49%)
  blocking collectives  65.9 us (32%)
  between operations  14.9 us (7%)
  matrix products  10.6 us (5%)
  starting transfers between devices  9.26 us (5%)
  local copies, waits for them, and re-layouts  2.63 us (1%)
    psum x1, waiting for transfers between devices, from_root(): return lax.psum(block, axis)  85.3 us
    all_gather x1, blocking collectives, on_device(): lax.all_gather(pair_weights.astype(jnp.bfloat16), 'pair', axis=0, tiled=T...  65.9 us
    all_gather x1, waiting for transfers between devices, on_device(): rows_piece = lax.all_gather(pair_slab, 'pair', axis=0, tiled=True)  13.9 us
    dot_general x1, matrix products, contract_pairs(): lax.dot_general(left, right, (((0,), (0,)), ((), ())), preferred_element_...  10.6 us
    all_to_all x1, starting transfers between devices, on_device(): lax.all_to_all(column_block, 'pair', split_axis=1, concat_axis=0, tiled=T...  9.21 us
  transfers between devices with their start and end apart: 3, of which 2 were waited for; matrix products, arithmetic and copies ran while one was open for 0% of the time, Pallas kernels for 0%

commit v1 on v0

v1 whole, which is shorter than its diff:
```python
import functools
import jax
import jax.numpy as jnp
from jax import lax
from jax.experimental import pallas as pl
from jax.experimental.pallas import tpu as pltpu
from jax.sharding import PartitionSpec as P

MESH = pl.DeviceIdType.MESH
NX, NY, NZ, NYL = 4, 8, 8, 4
DEPTH, ROWS, COLS = 384, 2048, 256
QUARTER, UNIT = ROWS // 4, DEPTH // 4

SLOTS = (
    (0, 1, 1), (0, 2, 1), (0, 1, 0), (1, 1, 1), (0, 3, 1), (0, 2, 0),
    (0, 0, 1), (1, 2, 1), (0, 3, 0), (1, 3, 1), (0, 0, 0), (1, 0, 1),
)
N = len(SLOTS)
START = (0, 1, 2)
AFTER = {1: (3, 4, 5, 6), 4: (7, 8), 6: (9, 10, 11)}
LAST = 13
CHUNKS = 16
PIECES = {
    7: ((0, 0), (0, 1)),
    8: ((0, 2), (0, 3)),
    11: ((-1, 0), (1, 0)),
    12: ((-1, 1), (1, -1), (-1, 2), (1, -2), (-1, 3), (1, -3)),
    13: ((2, 0), (2, 2), (2, 1), (2, 3)),
}
READY = {7: 0, 11: 1, 13: 2}


def mod(value, n):
    return lax.rem(value + 4 * n, n)


def kernel(slab, weight, out, panel, cols, scaled, wbuf, local, ysend, yrecv, xsend, xrecv, osend, orecv,
           sysend, syrecv, sxsend, sxrecv, zsend, zrecv, wsend, wrecv):
    z, col, pair = lax.axis_index("row"), lax.axis_index("col"), lax.axis_index("pair")
    x, yh, yl, c = col // 2, lax.rem(col, 2), pair // 2, lax.rem(pair, 2)
    y = yh * NYL + yl
    half = lax.rem(x, 2)

    def device(xx, yy, zz, cc):
        xx, yy, zz = mod(xx, NX), mod(yy, NY), mod(zz, NZ)
        return (zz, xx * 2 + yy // NYL, lax.rem(yy, NYL) * 2 + cc)

    ys = (device(x, y + 1, z, c), device(x, y - 1, z, c))
    xs = (device(x + 1, y, z, c), device(x - 1, y, z, c))
    zs = (device(x, y, z + 1, c), device(x, y, z - 1, c))
    sibling = device(x, y, z, 1 - c)

    def block(rel, flip):
        core = c + flip - 2 * c * flip
        return mod(yl + rel, NYL) * 2 + core

    def rows_at(rel, flip, group):
        return pl.ds(pl.multiple_of(block(rel, flip) * DEPTH + group * UNIT, 32), UNIT)

    def quarter_at(rel):
        return pl.ds(pl.multiple_of(mod(yl + rel, 4) * QUARTER, QUARTER), QUARTER)

    def unit(rel, flip, q, group):
        return panel.at[rows_at(rel, flip, group), quarter_at(q)]

    def remote(src, dst, send, recv, to):
        return pltpu.make_async_remote_copy(
            src_ref=src, dst_ref=dst, send_sem=send, recv_sem=recv, device_id=to, device_id_type=MESH
        )

    def group_of(d, low, own_half=True):
        return 2 * (half if own_half else 1 - half) + (low if d == 0 else 1 - low)

    def y_out(d, t):
        sign = 1 - 2 * d
        kind, q, low = SLOTS[t]
        piece = unit(-sign * kind, 0, sign * q, group_of(d, low))
        return remote(piece, piece, ysend.at[d, t], yrecv.at[d, t], ys[d])

    def arrived(d, t, own_half=True, flip=0):
        sign = 1 - 2 * d
        kind, q, low = SLOTS[t]
        return unit(-sign * (1 + kind), flip, sign * (q - 1), group_of(d, low, own_half))

    def y_in(d, t):
        piece = arrived(d, t)
        return remote(piece, piece, ysend.at[d, t], yrecv.at[d, t], ys[1 - d])

    def side(e, t):
        low = SLOTS[t][2]
        return 0 if low == e else 1

    def x_out(e, t):
        piece = arrived(side(e, t), t)
        return remote(piece, piece, xsend.at[e, t], xrecv.at[e, t], xs[e])

    def x_in(e, t):
        piece = arrived(side(e, t), t, own_half=False)
        return remote(piece, piece, xsend.at[e, t], xrecv.at[e, t], xs[1 - e])

    def sy(d, t, flip):
        piece = arrived(d, t, flip=flip)
        return remote(piece, piece, sysend.at[d, t], syrecv.at[d, t], sibling)

    def sx(e, t, flip):
        piece = arrived(side(e, t), t, own_half=False, flip=flip)
        return remote(piece, piece, sxsend.at[e, t], sxrecv.at[e, t], sibling)

    def own(q, flip):
        piece = panel.at[pl.ds(pl.multiple_of(block(0, flip) * DEPTH, DEPTH), DEPTH), quarter_at(q)]
        return remote(piece, piece, osend.at[q], orecv.at[q], sibling)

    def weights(n, rel, flip, to):
        piece = wbuf.at[block(rel, flip)]
        return remote(piece, piece, wsend.at[n], wrecv.at[n], to)

    column = pl.ds(pl.multiple_of(pair * COLS, COLS), COLS)
    distance = (mod(z - col, NZ), mod(col - z, NZ))

    def chunk(d, j, i):
        m = j // 2
        later = (m + 2) // 3
        sign = 1 - 2 * d
        rel = sign * (m + m // 2 - 2 * (m // 3))
        flip = (1 - later) * lax.rem(j, 2) + later * i
        part = (1 - later) * i + later * lax.rem(half + j, 2)
        return rows_at(rel, flip, 2 * part + d)

    def z_step(t, i):
        for d in range(2):
            j = t + 1 - distance[d]

            @pl.when((j >= 0) & (j < CHUNKS // 2))
            def _(d=d, j=j):
                rows = chunk(d, j, i)
                k = 2 * j + i

                @pl.when(distance[d] == 0)
                def _():
                    remote(panel.at[rows, column], cols.at[rows], zsend.at[d, k], zrecv.at[d, k], zs[d]).start()

                @pl.when(distance[d] > 0)
                def _():
                    remote(cols.at[rows], cols.at[rows], zsend.at[d, k], zrecv.at[d, k], zs[1 - d]).wait_recv()

                    @pl.when(distance[d] < NZ - 1)
                    def _():
                        remote(cols.at[rows], cols.at[rows], zsend.at[d, k], zrecv.at[d, k], zs[d]).start()

    def scale(rel):
        first = mod(yl + rel, NYL) * 2
        for b in range(2):
            for i in range(DEPTH // 128):
                at = pl.multiple_of((first + b) * DEPTH + i * 128, 128)
                w = wbuf[first + b, pl.ds(i, 1), :]

                @pl.when(z == col)
                def _(at=at, w=w):
                    tile = panel[pl.ds(at, 128), column].astype(jnp.float32)
                    scaled[:, pl.ds(at, 128)] = (jnp.transpose(tile) * w).astype(jnp.bfloat16)

                @pl.when(z != col)
                def _(at=at, w=w):
                    tile = cols[pl.ds(at, 128), :].astype(jnp.float32)
                    scaled[:, pl.ds(at, 128)] = (jnp.transpose(tile) * w).astype(jnp.bfloat16)

    def multiply(rel, q):
        at = pl.ds(pl.multiple_of(mod(yl + rel, NYL) * 2 * DEPTH, 2 * DEPTH), 2 * DEPTH)
        where = quarter_at(q)
        value = jnp.dot(scaled[:, at], panel[at, where], preferred_element_type=jnp.float32)
        if rel == 0:
            out[:, where] = value
        else:
            out[:, where] += value

    mine = pltpu.make_async_copy(slab, panel.at[pl.ds(pl.multiple_of(pair * DEPTH, DEPTH), DEPTH)], local.at[0])
    mine.start()
    my_weights = pltpu.make_async_copy(weight, wbuf.at[pair], local.at[1])
    my_weights.start()
    barrier = pltpu.get_barrier_semaphore()
    partners = ys + xs + zs + (sibling,)
    for to in partners:
        pl.semaphore_signal(barrier, inc=1, device_id=to, device_id_type=MESH)
    mine.wait()
    my_weights.wait()
    pl.semaphore_wait(barrier, len(partners))

    for t in START:
        for d in range(2):
            y_out(d, t).start()
    own(0, 0).start()
    z_step(-1, 0)
    z_step(-1, 1)
    for q in range(1, 4):
        own(q, 0).start()
    weights(0, 0, 0, ys[0]).start()
    weights(1, 0, 0, ys[1]).start()
    weights(2, 0, 0, sibling).start()

    for t in range(LAST + 1):
        if t < N:
            for d in range(2):
                y_in(d, t).wait_recv()
            for s in AFTER.get(t, ())[:1]:
                for d in range(2):
                    y_out(d, s).start()
            for e in range(2):
                x_out(e, t).start()
            for s in AFTER.get(t, ())[1:]:
                for d in range(2):
                    y_out(d, s).start()
            for d in range(2):
                sy(d, t, 0).start()
        if t == 0:
            own(0, 1).wait_recv()
        if 1 <= t <= N:
            for d in range(2):
                sy(d, t - 1, 1).wait_recv()
        z_step(t, 0)
        if 1 <= t <= N:
            for e in range(2):
                x_in(e, t - 1).wait_recv()
                sx(e, t - 1, 0).start()
        if 2 <= t <= N + 1:
            for e in range(2):
                sx(e, t - 2, 1).wait_recv()
        z_step(t, 1)
        if t == 1:
            weights(0, -1, 0, ys[1]).wait_recv()
            weights(1, 1, 0, ys[0]).wait_recv()
            weights(2, 0, 1, sibling).wait_recv()
            weights(3, -1, 0, ys[0]).start()
            weights(4, -1, 0, sibling).start()
            weights(5, 1, 0, sibling).start()
        if t == 2:
            for q in range(1, 4):
                own(q, 1).wait_recv()
        if t == 4:
            weights(3, 2, 0, ys[1]).wait_recv()
            weights(6, 2, 0, sibling).start()
            weights(4, -1, 1, sibling).wait_recv()
            weights(5, 1, 1, sibling).wait_recv()
        if t == 6:
            weights(6, 2, 1, sibling).wait_recv()
        if t in READY:
            for rel in {0: (0,), 1: (-1, 1), 2: (2,)}[READY[t]]:
                scale(rel)
        for rel, q in PIECES.get(t, ()):
            multiply(rel, q)

    for t in range(N):
        for d in range(2):
            y_out(d, t).wait_send()
            x_out(d, t).wait_send()
            sy(d, t, 0).wait_send()
            sx(d, t, 0).wait_send()
    for q in range(4):
        own(q, 0).wait_send()
    for n, (rel, to) in enumerate(((0, ys[0]), (0, ys[1]), (0, sibling), (-1, ys[0]), (-1, sibling), (1, sibling), (2, sibling))):
        weights(n, rel, 0, to).wait_send()
    for d in range(2):

        @pl.when(distance[d] < NZ - 1)
        def _(d=d):
            for k in range(CHUNKS):
                rows = pl.ds(k * UNIT, UNIT)
                remote(cols.at[rows], cols.at[rows], zsend.at[d, k], zrecv.at[d, k], zs[d]).wait_send()


def gather_and_multiply(slab, weight):
    dma = pltpu.SemaphoreType.DMA
    return pl.pallas_call(
        kernel,
        out_shape=jax.ShapeDtypeStruct((COLS, ROWS), jnp.float32),
        in_specs=[pl.BlockSpec(memory_space=pl.ANY)] * 2,
        out_specs=pl.BlockSpec(memory_space=pltpu.VMEM),
        scratch_shapes=[
            pltpu.VMEM((8 * DEPTH, ROWS), jnp.bfloat16),
            pltpu.VMEM((8 * DEPTH, COLS), jnp.bfloat16),
            pltpu.VMEM((COLS, 8 * DEPTH), jnp.bfloat16),
            pltpu.VMEM((8, DEPTH // 128, 128), jnp.float32),
            dma((2,)),
            dma((2, N)), dma((2, N)), dma((2, N)), dma((2, N)),
            dma((4,)), dma((4,)),
            dma((2, N)), dma((2, N)), dma((2, N)), dma((2, N)),
            dma((2, CHUNKS)), dma((2, CHUNKS)),
            dma((7,)), dma((7,)),
        ],
        compiler_params=pltpu.CompilerParams(collective_id=0, has_side_effects=True),
        cost_estimate=pl.CostEstimate(flops=2 * 8 * DEPTH * ROWS * COLS, bytes_accessed=4 << 20, transcendentals=0),
    )(slab, weight)


def on_device(pair_slab, pair_weights):
    return gather_and_multiply(pair_slab, pair_weights.reshape(DEPTH // 128, 128)).T


def solution(mesh):
    placed = (P("pair", "row"), P("pair"))
    return jax.shard_map(
        on_device, mesh=mesh, in_specs=placed, out_specs=P("row", ("col", "pair")), check_vma=False
    )
```

time: 205 us -> 69.8 us (0.34)
  the two profiles are of different devices: /device:TPU:9 before, /device:TPU:64 now
where the time goes in v1:
time: 69.8 us; the launch traced here: 69.6 us
  Pallas kernels  66.7 us (96%)
  local copies, waits for them, and re-layouts  2.89 us (4%)
    pallas_call x1, Pallas kernels, gather_and_multiply(): pl.pallas_call(kernel, out_shape=jax.ShapeDtypeStruct((COLS, ROWS), jnp.f...  66.7 us
    transpose x1, local copies, waits for them, and re-layouts, on_device(): gather_and_multiply(pair_slab, pair_weights.reshape(DEPTH // 128, 128))  2.89 us

profile of v1, /device:TPU:64, one launch (start us, length us, event | category | flops | bytes accessed | tf_op | source)
XLA Modules:
  0.0 69.6 jit_solution(9718605798199106874)
XLA Ops:
  0.0 66.7 %shard_map.28 = f32[256,2048]{1,0:T(8,128)} custom-call(bf16[384,2048]{1,0:T(8,128)(2,1)} %slab.1, f32[3,128]{1,0:T(4,128)} %bitcast.3), custom_call_target="tpu_custom_call" | custom-call | flops 3221225472 | bytes 4194304 | tf_op jit(solution)/shard_map/pallas_call | solution.py:272
  66.8 2.9 %copy.3 = f32[2048,256]{1,0:T(8,128)} copy(f32[2048,256]{0,1:T(8,128)} %bitcast.2) | data formatting | bytes 4194304 | tf_op jit(solution)/shard_map/transpose | solution.py:295

commit v2 on v1

v2 whole, which is shorter than its diff:
```python
import functools
import jax
import jax.numpy as jnp
from jax import lax
from jax.experimental import pallas as pl
from jax.experimental.pallas import tpu as pltpu
from jax.sharding import PartitionSpec as P

MESH = pl.DeviceIdType.MESH
NX, NY, NZ, NYL = 4, 8, 8, 4
DEPTH, ROWS, COLS = 384, 2048, 256
QUARTER, UNIT = ROWS // 4, DEPTH // 4

SLOTS = (
    (0, 1, 1), (0, 2, 1), (0, 1, 0), (1, 1, 1), (0, 3, 1), (0, 2, 0),
    (0, 0, 1), (1, 2, 1), (0, 3, 0), (1, 3, 1), (0, 0, 0), (1, 0, 1),
)
N = len(SLOTS)
FLIGHT = 5
XL = SL = 4

UNITS, ONE_WAY = 11, 5
CHUNKS = 2 * UNITS
BLOCK = sum(v << (2 * n) for n, v in enumerate((0, 0, 1, 3, 1, 2, 2, 3, 3, 2, 2)))
PART = sum(v << (2 * n) for n, v in enumerate((0, 1, 2, 2, 3, 2, 2, 3, 3, 3, 3)))
OTHER = sum(v << (2 * n) for n, v in enumerate((0, 0, 0, 0, 0, 0, 1, 0, 1, 0, 1)))
REACH = (4, 3)
NEEDS = {0: (0, 1), 1: (2, 3, 4, 7, 8), 2: (5, 6, 9, 10)}
HOP = 3
LAST = 20 + HOP * 4
PRODUCTS = {
    22: ((0, 0),), 23: ((0, 2),), 24: ((0, 1),), 25: ((0, 3),),
    29: ((-1, 0), (1, 0), (-1, 1), (1, 3)), 30: ((-1, 2), (1, 2)), 31: ((-1, 3), (1, 1)),
    LAST: ((2, 0), (2, 2), (2, 1), (2, 3)),
}
SCALES = {22: (0,), 29: (-1, 1), LAST: (2,)}


def schedule():
    after, last = {}, -1
    for s in range(2 * N):
        kind, q, low = SLOTS[s // 2]
        need = s - FLIGHT
        if kind:
            need = max(need, 2 * SLOTS.index((0, (q + 1) % 4, low)) + s % 2)
        last = max(last, need)
        after.setdefault(last, []).append(s)
    return after


def mod(value, n):
    return lax.rem(value + 4 * n, n)


def kernel(slab, weight, out, panel, ring, other, scaled, wbuf, local, ysend, yrecv, xsend, xrecv, osend, orecv,
           sysend, syrecv, sxsend, sxrecv, zsend, zrecv, hsend, hrecv, wsend, wrecv):
    z, col, pair = lax.axis_index("row"), lax.axis_index("col"), lax.axis_index("pair")
    x, yh, yl, c = col // 2, lax.rem(col, 2), pair // 2, lax.rem(pair, 2)
    y = yh * NYL + yl
    half = lax.rem(x, 2)

    def device(xx, yy, zz, cc):
        xx, yy, zz = mod(xx, NX), mod(yy, NY), mod(zz, NZ)
        return (zz, xx * 2 + yy // NYL, lax.rem(yy, NYL) * 2 + cc)

    ys = (device(x, y + 1, z, c), device(x, y - 1, z, c))
    xs = (device(x + 1, y, z, c), device(x - 1, y, z, c))
    zs = (device(x, y, z + 1, c), device(x, y, z - 1, c))
    sibling = device(x, y, z, 1 - c)

    def block(rel, flip):
        core = c + flip - 2 * c * flip
        return mod(yl + rel, NYL) * 2 + core

    def rows_at(rel, flip, group):
        return pl.ds(pl.multiple_of(block(rel, flip) * DEPTH + group * UNIT, 32), UNIT)

    def quarter_at(rel):
        return pl.ds(pl.multiple_of(mod(yl + rel, 4) * QUARTER, QUARTER), QUARTER)

    def unit(rel, flip, q, group, h=None):
        if h is None:
            return panel.at[rows_at(rel, flip, group), quarter_at(q)]
        first = block(rel, flip) * DEPTH + group * UNIT + h * (UNIT // 2)
        return panel.at[pl.ds(pl.multiple_of(first, 16), UNIT // 2), quarter_at(q)]

    def remote(src, dst, send, recv, to):
        return pltpu.make_async_remote_copy(
            src_ref=src, dst_ref=dst, send_sem=send, recv_sem=recv, device_id=to, device_id_type=MESH
        )

    def group_of(d, low, own_half=True):
        return 2 * (half if own_half else 1 - half) + (low if d == 0 else 1 - low)

    def y_out(d, u):
        sign = 1 - 2 * d
        kind, q, low = SLOTS[u // 2]
        piece = unit(-sign * kind, 0, sign * q, group_of(d, low), u % 2)
        return remote(piece, piece, ysend.at[d, u], yrecv.at[d, u], ys[d])

    def arrived(d, t, own_half=True, flip=0, h=None):
        sign = 1 - 2 * d
        kind, q, low = SLOTS[t]
        return unit(-sign * (1 + kind), flip, sign * (q - 1), group_of(d, low, own_half), h)

    def y_in(d, u):
        piece = arrived(d, u // 2, h=u % 2)
        return remote(piece, piece, ysend.at[d, u], yrecv.at[d, u], ys[1 - d])

    def side(e, t):
        low = SLOTS[t][2]
        return 0 if low == e else 1

    def x_out(e, u):
        piece = arrived(side(e, u // 2), u // 2, h=u % 2)
        return remote(piece, piece, xsend.at[e, u], xrecv.at[e, u], xs[e])

    def x_in(e, u):
        piece = arrived(side(e, u // 2), u // 2, own_half=False, h=u % 2)
        return remote(piece, piece, xsend.at[e, u], xrecv.at[e, u], xs[1 - e])

    def sy(d, t, flip):
        piece = arrived(d, t, flip=flip)
        return remote(piece, piece, sysend.at[d, t], syrecv.at[d, t], sibling)

    def sx(e, t, flip):
        piece = arrived(side(e, t), t, own_half=False, flip=flip)
        return remote(piece, piece, sxsend.at[e, t], sxrecv.at[e, t], sibling)

    def own(q, flip):
        piece = panel.at[pl.ds(pl.multiple_of(block(0, flip) * DEPTH, DEPTH), DEPTH), quarter_at(q)]
        return remote(piece, piece, osend.at[q], orecv.at[q], sibling)

    def weights(n, rel, flip, to):
        piece = wbuf.at[block(rel, flip)]
        return remote(piece, piece, wsend.at[n], wrecv.at[n], to)

    column = pl.ds(pl.multiple_of(pair * COLS, COLS), COLS)
    distance = (mod(z - col, NZ), mod(col - z, NZ))

    wide = quarter_at(0)
    left = pl.ds(pl.multiple_of(c * COLS, COLS), COLS)
    right = pl.ds(pl.multiple_of((1 - c) * COLS, COLS), COLS)

    def ring_rows(d, n, h=None):
        swap = (OTHER >> (2 * n)) & 1
        group = swap if d == 0 else 1 - swap
        rel = mod(yl + (1 - 2 * group) * ((BLOCK >> (2 * n)) & 3), NYL)
        code = (PART >> (2 * n)) & 3
        by_half = code // 2
        part = by_half * lax.rem(half + code, 2) + (1 - by_half) * code
        inside = (2 * part + group) * UNIT
        if h is None:
            return pl.ds(pl.multiple_of(rel * DEPTH + inside, 32), UNIT)
        inside = inside + h * (UNIT // 2)
        return tuple(pl.ds(pl.multiple_of(first * DEPTH + inside, 16), UNIT // 2) for first in (rel, 2 * rel + c))

    def hand_over(d, n):
        rows = ring_rows(d, n)
        return remote(ring.at[rows, right], other.at[rows], hsend.at[d, n], hrecv.at[d, n], sibling)

    def hand_in(d, n):
        rows = ring_rows(d, n)
        return remote(other.at[rows], other.at[rows], hsend.at[d, n], hrecv.at[d, n], sibling)

    def reaches(d, n):
        reach = NZ - 1 if n < ONE_WAY else REACH[d]
        return (distance[d] > 0) & (distance[d] <= reach), distance[d] < reach

    def z_step(u):
        for d in range(2):
            w = u - HOP * distance[d]
            late = (w + 64) // 69
            k = w + 2 - late

            @pl.when((w >= -2) & (w != 4) & (k < CHUNKS))
            def _(d=d, k=k):
                n, h = k // 2, lax.rem(k, 2)
                rows, source_rows = ring_rows(d, n, h)
                reach = NZ - 1 - (NZ - 1 - REACH[d]) * jnp.minimum(k // (2 * ONE_WAY), 1)
                sems = zsend.at[d, k], zrecv.at[d, k]

                @pl.when(distance[d] == 0)
                def _():
                    remote(panel.at[source_rows, wide], ring.at[rows], *sems, zs[d]).start()

                @pl.when((distance[d] > 0) & (distance[d] <= reach))
                def _():
                    remote(ring.at[rows], ring.at[rows], *sems, zs[1 - d]).wait_recv()

                    @pl.when(distance[d] < reach)
                    def _():
                        remote(ring.at[rows], ring.at[rows], *sems, zs[d]).start()

                    @pl.when(h == 1)
                    def _():
                        hand_over(d, n).start()

    def scale(rel):
        for n in NEEDS[abs(rel)]:
            for d in range(2):
                if rel == -1:

                    @pl.when(reaches(d, n)[0])
                    def _(d=d, n=n):
                        hand_in(d, n).wait_recv()

                elif rel != 1:

                    @pl.when(reaches(d, n)[0])
                    def _(d=d, n=n):
                        hand_in(d, n).wait_recv()

        first = mod(yl + rel, NYL)
        for flip in range(2):
            b = block(rel, flip)
            for i in range(DEPTH // 128):
                at = pl.multiple_of(b * DEPTH + i * 128, 128)
                rows = pl.ds(pl.multiple_of(first * DEPTH + i * 128, 128), 128)
                w = wbuf[b, pl.ds(i, 1), :]

                @pl.when(z == col)
                def _(at=at, w=w):
                    tile = panel[pl.ds(at, 128), column].astype(jnp.float32)
                    scaled[:, pl.ds(at, 128)] = (jnp.transpose(tile) * w).astype(jnp.bfloat16)

                @pl.when(z != col)
                def _(at=at, w=w, rows=rows, flip=flip):
                    tile = (other[rows, :] if flip else ring[rows, left]).astype(jnp.float32)
                    scaled[:, pl.ds(at, 128)] = (jnp.transpose(tile) * w).astype(jnp.bfloat16)

    def multiply(rel, q):
        at = pl.ds(pl.multiple_of(mod(yl + rel, NYL) * 2 * DEPTH, 2 * DEPTH), 2 * DEPTH)
        where = quarter_at(q)
        value = jnp.dot(scaled[:, at], panel[at, where], preferred_element_type=jnp.float32)
        if rel == 0:
            out[:, where] = value
        else:
            out[:, where] += value

    mine = pltpu.make_async_copy(slab, panel.at[pl.ds(pl.multiple_of(pair * DEPTH, DEPTH), DEPTH)], local.at[0])
    mine.start()
    my_weights = pltpu.make_async_copy(weight, wbuf.at[pair], local.at[1])
    my_weights.start()
    barrier = pltpu.get_barrier_semaphore()
    partners = ys + xs + zs + (sibling,)
    for to in partners:
        pl.semaphore_signal(barrier, inc=1, device_id=to, device_id_type=MESH)
    mine.wait()
    my_weights.wait()
    pl.semaphore_wait(barrier, len(partners))

    after = schedule()
    for s in after[-1]:
        for d in range(2):
            y_out(d, s).start()
    own(0, 0).start()
    z_step(-2)
    z_step(-1)
    for q in range(1, 4):
        own(q, 0).start()
    weights(0, 0, 0, ys[0]).start()
    weights(1, 0, 0, ys[1]).start()
    weights(2, 0, 0, sibling).start()

    for u in range(LAST + 1):
        if u < 2 * N:
            for d in range(2):
                y_in(d, u).wait_recv()
            for s in after.get(u, ()):
                for d in range(2):
                    y_out(d, s).start()
            for e in range(2):
                x_out(e, u).start()
            if u % 2:
                for d in range(2):
                    sy(d, u // 2, 0).start()
        if u == 0:
            own(0, 1).wait_recv()
        if u % 2 and 0 <= u - 1 - SL < 2 * N:
            for d in range(2):
                sy(d, (u - 1 - SL) // 2, 1).wait_recv()
        if 0 <= u - XL < 2 * N:
            for e in range(2):
                x_in(e, u - XL).wait_recv()
            if u % 2:
                for e in range(2):
                    sx(e, (u - 1 - XL) // 2, 0).start()
        if u % 2 and 0 <= u - 1 - XL - SL < 2 * N:
            for e in range(2):
                sx(e, (u - 1 - XL - SL) // 2, 1).wait_recv()
        z_step(u)
        if u == 2:
            weights(0, -1, 0, ys[1]).wait_recv()
            weights(1, 1, 0, ys[0]).wait_recv()
            weights(2, 0, 1, sibling).wait_recv()
            weights(3, -1, 0, ys[0]).start()
            weights(4, -1, 0, sibling).start()
            weights(5, 1, 0, sibling).start()
        if u == 4:
            for q in range(1, 4):
                own(q, 1).wait_recv()
        if u == 8:
            weights(3, 2, 0, ys[1]).wait_recv()
            weights(6, 2, 0, sibling).start()
            weights(4, -1, 1, sibling).wait_recv()
            weights(5, 1, 1, sibling).wait_recv()
        if u == 12:
            weights(6, 2, 1, sibling).wait_recv()
        for rel in SCALES.get(u, ()):
            scale(rel)
        for rel, q in PRODUCTS.get(u, ()):
            multiply(rel, q)

    for u in range(2 * N):
        for d in range(2):
            y_out(d, u).wait_send()
            x_out(d, u).wait_send()
    for t in range(N):
        for d in range(2):
            sy(d, t, 0).wait_send()
            sx(d, t, 0).wait_send()
    for q in range(4):
        own(q, 0).wait_send()
    for n, (rel, to) in enumerate(((0, ys[0]), (0, ys[1]), (0, sibling), (-1, ys[0]), (-1, sibling), (1, sibling), (2, sibling))):
        weights(n, rel, 0, to).wait_send()
    for d in range(2):
        for low, high in ((0, ONE_WAY), (ONE_WAY, UNITS)):

            @pl.when(reaches(d, low)[1])
            def _(d=d, low=low, high=high):
                for k in range(2 * low, 2 * high):
                    rows = pl.ds(0, UNIT // 2)
                    remote(ring.at[rows], ring.at[rows], zsend.at[d, k], zrecv.at[d, k], zs[d]).wait_send()

            @pl.when(reaches(d, low)[0])
            def _(d=d, low=low, high=high):
                for n in range(low, high):
                    hand_over(d, n).wait_send()


def gather_and_multiply(slab, weight):
    dma = pltpu.SemaphoreType.DMA
    return pl.pallas_call(
        kernel,
        out_shape=jax.ShapeDtypeStruct((COLS, ROWS), jnp.float32),
        in_specs=[pl.BlockSpec(memory_space=pltpu.HBM)] * 2,
        out_specs=pl.BlockSpec(memory_space=pltpu.VMEM),
        scratch_shapes=[
            pltpu.VMEM((8 * DEPTH, ROWS), jnp.bfloat16),
            pltpu.VMEM((4 * DEPTH, 2 * COLS), jnp.bfloat16),
            pltpu.VMEM((4 * DEPTH, COLS), jnp.bfloat16),
            pltpu.VMEM((COLS, 8 * DEPTH), jnp.bfloat16),
            pltpu.VMEM((8, DEPTH // 128, 128), jnp.float32),
            dma((2,)),
            dma((2, 2 * N)), dma((2, 2 * N)), dma((2, 2 * N)), dma((2, 2 * N)),
            dma((4,)), dma((4,)),
            dma((2, N)), dma((2, N)), dma((2, N)), dma((2, N)),
            dma((2, CHUNKS)), dma((2, CHUNKS)),
            dma((2, UNITS)), dma((2, UNITS)),
            dma((7,)), dma((7,)),
        ],
        compiler_params=pltpu.CompilerParams(collective_id=0, has_side_effects=True, vmem_limit_bytes=30 << 20),
        cost_estimate=pl.CostEstimate(flops=2 * 8 * DEPTH * ROWS * COLS, bytes_accessed=4 << 20, transcendentals=0),
    )(slab, weight)


def on_device(pair_slab, pair_weights):
    return gather_and_multiply(pair_slab, pair_weights.reshape(DEPTH // 128, 128)).T


def solution(mesh):
    placed = (P("pair", "row"), P("pair"))
    return jax.shard_map(
        on_device, mesh=mesh, in_specs=placed, out_specs=P("row", ("col", "pair")), check_vma=False
    )
```

time: 69.8 us -> 64.5 us (0.924)
  the two profiles are of different devices: /device:TPU:64 before, /device:TPU:5 now
where the time goes in v2:
time: 64.5 us; the launch traced here: 64.3 us
  Pallas kernels  60.4 us (94%)
  local copies, waits for them, and re-layouts  3.9 us (6%)
    pallas_call x1, Pallas kernels, gather_and_multiply(): pl.pallas_call(kernel, out_shape=jax.ShapeDtypeStruct((COLS, ROWS), jnp.f...  60.4 us
    unnamed x4, local copies, waits for them, and re-layouts  2.09 us
    transpose x1, local copies, waits for them, and re-layouts, on_device(): gather_and_multiply(pair_slab, pair_weights.reshape(DEPTH // 128, 128))  1.81 us

profile of v2, /device:TPU:5, one launch (start us, length us, event | category | flops | bytes accessed | tf_op | source)
XLA Modules:
  0.0 64.3 jit_solution(5202302096578562710)
XLA Ops:
  0.0 0.0 copy-start
  0.0 1.4 %copy-done = bf16[384,2048]{1,0:T(8,128)(2,1)S(1)} copy-done((bf16[384,2048]{1,0:T(8,128)(2,1)S(1)}, bf16[384,2048]{1,0:T(8,128)(2,1)}, u32[]{:S(2)}) %copy-start) | copy-done | bytes 1572888
  1.4 0.0 copy-start.1
  1.4 0.7 %copy-done.1 = f32[384]{0:T(512)S(1)} copy-done((f32[384]{0:T(512)S(1)}, f32[384]{0:T(512)}, u32[]{:S(2)}) %copy-start.1) | copy-done | bytes 1560
  2.1 60.4 %shard_map.28 = f32[256,2048]{1,0:T(8,128)S(1)} custom-call(bf16[384,2048]{1,0:T(8,128)(2,1)S(1)} %copy-done, f32[3,128]{1,0:T(4,128)S(1)} %bitcast.3), custom_call_target="tpu_custom_call" | custom-call | flops 3221225472 | bytes 4194304 | tf_op jit(solution)/shard_map/pallas_call | solution.py:344
  62.5 1.8 %copy.3 = f32[2048,256]{1,0:T(8,128)} copy(f32[2048,256]{0,1:T(8,128)S(1)} %bitcast.2) | data formatting | bytes 4194304 | tf_op jit(solution)/shard_map/transpose | solution.py:369
Async XLA Ops:
  0.0 1.4 %copy-start = (bf16[384,2048]{1,0:T(8,128)(2,1)S(1)}, bf16[384,2048]{1,0:T(8,128)(2,1)}, u32[]{:S(2)}) copy-start(bf16[384,2048]{1,0:T(8,128)(2,1)} %slab.1) | copy-start | bytes 4718596
  1.4 0.7 %copy-start.1 = (f32[384]{0:T(512)S(1)}, f32[384]{0:T(512)}, u32[]{:S(2)}) copy-start(f32[384]{0:T(512)} %param.3) | copy-start | bytes 4612

commit v3 on v2

--- a/solution.py
+++ b/solution.py
@@ -362,7 +362,7 @@
         ],
         compiler_params=pltpu.CompilerParams(collective_id=0, has_side_effects=True, vmem_limit_bytes=30 << 20),
         cost_estimate=pl.CostEstimate(flops=2 * 8 * DEPTH * ROWS * COLS, bytes_accessed=4 << 20, transcendentals=0),
-    )(slab, weight)
+    )(pltpu.with_memory_space_constraint(slab, pltpu.HBM), pltpu.with_memory_space_constraint(weight, pltpu.HBM))
 
 
 def on_device(pair_slab, pair_weights):

time: 64.5 us -> 62.3 us (0.966)
  local copies, waits for them, and re-layouts: 3.9 us -> 1.81 us
    unnamed x4 -> x0, local copies, waits for them, and re-layouts: 2.09 us -> none
where the time goes in v3:
time: 62.3 us; the launch traced here: 62.1 us
  Pallas kernels  60.3 us (97%)
  local copies, waits for them, and re-layouts  1.81 us (3%)
    pallas_call x1, Pallas kernels, gather_and_multiply(): pl.pallas_call(kernel, out_shape=jax.ShapeDtypeStruct((COLS, ROWS), jnp.f...  60.3 us
    transpose x1, local copies, waits for them, and re-layouts, on_device(): gather_and_multiply(pair_slab, pair_weights.reshape(DEPTH // 128, 128))  1.81 us

profile of v3, /device:TPU:5, one launch (start us, length us, event | category | flops | bytes accessed | tf_op | source)
XLA Modules:
  0.0 62.1 jit_solution(17988066843398536236)
XLA Ops:
  0.0 60.3 %shard_map.28 = f32[256,2048]{1,0:T(8,128)S(1)} custom-call(bf16[384,2048]{1,0:T(8,128)(2,1)} %slab.1, f32[3,128]{1,0:T(4,128)} %bitcast.3), custom_call_target="tpu_custom_call" | custom-call | flops 3221225472 | bytes 4194304 | tf_op jit(solution)/shard_map/pallas_call | solution.py:344
  60.3 1.8 %copy.3 = f32[2048,256]{1,0:T(8,128)} copy(f32[2048,256]{0,1:T(8,128)S(1)} %bitcast.2) | data formatting | bytes 4194304 | tf_op jit(solution)/shard_map/transpose | solution.py:369

commit v4 on v3

--- a/solution.py
+++ b/solution.py
@@ -27,13 +27,13 @@
 REACH = (4, 3)
 NEEDS = {0: (0, 1), 1: (2, 3, 4, 7, 8), 2: (5, 6, 9, 10)}
 HOP = 3
-LAST = 20 + HOP * 4
+LAST = 19 + HOP * 4
 PRODUCTS = {
-    22: ((0, 0),), 23: ((0, 2),), 24: ((0, 1),), 25: ((0, 3),),
-    29: ((-1, 0), (1, 0), (-1, 1), (1, 3)), 30: ((-1, 2), (1, 2)), 31: ((-1, 3), (1, 1)),
+    21: ((0, 0),), 22: ((0, 2),), 23: ((0, 1),), 24: ((0, 3),),
+    28: ((-1, 0), (1, 0), (-1, 1), (1, 3)), 29: ((-1, 2), (1, 2)), 30: ((-1, 3), (1, 1)),
     LAST: ((2, 0), (2, 2), (2, 1), (2, 3)),
 }
-SCALES = {22: (0,), 29: (-1, 1), LAST: (2,)}
+SCALES = {21: (0,), 28: (-1, 1), LAST: (2,)}
 
 
 def schedule():
@@ -169,7 +169,7 @@
 
     def z_step(u):
         for d in range(2):
-            w = u - HOP * distance[d]
+            w = u - HOP * distance[d] + jnp.minimum(distance[d], 1)
             late = (w + 64) // 69
             k = w + 2 - late
 

time: 62.3 us -> 61.5 us (0.987)
  the two profiles are of different devices: /device:TPU:5 before, /device:TPU:65 now
where the time goes in v4:
time: 61.5 us; the launch traced here: 61.3 us
  Pallas kernels  59.5 us (97%)
  local copies, waits for them, and re-layouts  1.81 us (3%)
    pallas_call x1, Pallas kernels, gather_and_multiply(): pl.pallas_call(kernel, out_shape=jax.ShapeDtypeStruct((COLS, ROWS), jnp.f...  59.5 us
    transpose x1, local copies, waits for them, and re-layouts, on_device(): gather_and_multiply(pair_slab, pair_weights.reshape(DEPTH // 128, 128))  1.81 us

profile of v4, /device:TPU:65, one launch (start us, length us, event | category | flops | bytes accessed | tf_op | source)
XLA Modules:
  0.0 61.3 jit_solution(13208239252420829379)
XLA Ops:
  0.0 59.5 %shard_map.28 = f32[256,2048]{1,0:T(8,128)S(1)} custom-call(bf16[384,2048]{1,0:T(8,128)(2,1)} %slab.1, f32[3,128]{1,0:T(4,128)} %bitcast.3), custom_call_target="tpu_custom_call" | custom-call | flops 3221225472 | bytes 4194304 | tf_op jit(solution)/shard_map/pallas_call | solution.py:344
  59.5 1.8 %copy.3 = f32[2048,256]{1,0:T(8,128)} copy(f32[2048,256]{0,1:T(8,128)S(1)} %bitcast.2) | data formatting | bytes 4194304 | tf_op jit(solution)/shard_map/transpose | solution.py:369
